TPU v7x, 32 devices: a whole 2x2x4 slice. The times are simulated.
32 devices in a mesh: dp: 2 (over y), seq: 8 (over z, x), head: 2 (over core).
Axes of the slice: x: 2, y: 2, z: 4, core: 2. Of those that a mesh axis runs over, the one named last changes fastest.
Arguments:
- queries: bfloat16 [128, 8, 1024], P('seq', 'dp', 'head'), parts along dimension 1, may hold values from -6 to 6
- gate_pre: bfloat16 [128, 8, 1024], P('seq', 'dp', 'head'), parts along dimension 1, may hold values from -6 to 6
- event_keys: bfloat16 [8192, 8, 1024], P('seq', 'dp', 'head'), parts along dimension 1, may hold values from -6 to 6
- event_values: bfloat16 [8192, 8, 1024], P('seq', 'dp', 'head'), parts along dimension 1, may hold values from -6 to 6
- block_lists: int32 [8, 8, 4], P(None, 'dp'), parts along dimension 1, may hold values from 0 to 7, all different within a row; in each aligned block of 4 rows (0 to 3, 4 to 7, ..., all dimensions but the last counted through in order) at most 2 rows name the same one
- history_len: int32 [8], P('dp'), parts along dimension 0, may hold values from 4 to 8
- out_grad: bfloat16 [128, 8, 1024], P('seq', 'dp', 'head'), parts along dimension 1, may hold values from -6 to 6
Outputs:
- layer_out: bfloat16 [128, 8, 1024], P('seq', 'dp', 'head'), parts along dimension 1
- grad_queries: bfloat16 [128, 8, 1024], P('seq', 'dp', 'head'), parts along dimension 1
- grad_gate: bfloat16 [128, 8, 1024], P('seq', 'dp', 'head'), parts along dimension 1
- grad_keys: bfloat16 [8192, 8, 1024], P('seq', 'dp', 'head'), parts along dimension 1
- grad_values: bfloat16 [8192, 8, 1024], P('seq', 'dp', 'head'), parts along dimension 1
There are 2 independent parts, one for each index of `dp`. A program takes and returns all parts, laid end to end along the dimension named above; each array names one. Nothing has to cross between parts.
Inputs may be any that keep to these rules, and one draw needn't show every extreme that they name: Latent span c of user u names blocks (c - block_lists[c, u, i]) mod 8; the 4 entries of one row differ. Among the 4 rows of one latent span no offset occurs in more than 2 rows, and in some latent span one offset occurs in exactly 2 rows.
All inputs are finite; a program needn't handle non-finite values.
Results may differ from a plain program's by a relative error of at most 0.014.
Values may be sent and summed in bfloat16 or wider, within the bound.
A program may use at most 192 MiB of HBM per device.

v0:
```python
import functools

import jax
import jax.numpy as jnp
from jax import lax
from jax.experimental import pallas as pl
from jax.experimental.pallas import tpu as pltpu
from jax.sharding import PartitionSpec as P

HEAD_DIM = 64
EPS = 1e-06
SLOTS = 2
PAIR = 2 * HEAD_DIM
TILE = 256
F32 = jnp.float32
BF16 = jnp.bfloat16
NT = (((1,), (1,)), ((), ()))
NN = (((1,), (0,)), ((), ()))


def dot(a, b, dims):
    return lax.dot_general(a, b, dims, preferred_element_type=F32)


def split_heads(rows):
    lane = lax.broadcasted_iota(jnp.int32, rows.shape, 1)
    zero = jnp.zeros_like(rows)
    return jnp.concatenate(
        [jnp.where(lane < HEAD_DIM, rows, zero), jnp.where(lane < HEAD_DIM, zero, rows)], axis=0
    )


def join_heads(flipped):
    half = flipped.shape[1] // 2
    return jnp.concatenate([flipped[:HEAD_DIM, :half], flipped[HEAD_DIM:, half:]], axis=0).T


def kernel(n, chunks, lists, lens, small, keys, values, small_out, dkeys, dvalues,
           k_buf, v_buf, kt_buf, vt_buf, w_buf, s_buf, q_dense, d_dense, a_dense, g_dense, d_own,
           sends, recvs,
           user_hold, slot_hold, user_own, slot_own,
           send_sem, recv_sem, load_sem, store_sem):
    users, events, width = k_buf.shape
    rows = small.shape[2]
    wide = width // chunks
    pairs = wide // PAIR
    latents = n * rows
    me = lax.axis_index("seq")

    def load_copy(i, u):
        src, dst = ((keys, k_buf), (values, v_buf))[i]
        return pltpu.make_async_copy(src.at[u], dst.at[u], load_sem.at[i, u])

    for u in range(users):
        load_copy(0, u).start()
        load_copy(1, u).start()

    barrier = pltpu.get_barrier_semaphore()

    def greet(d, carry):
        pl.semaphore_signal(barrier, inc=1, device_id={"seq": lax.rem(me + d, n)},
                            device_id_type=pl.DeviceIdType.MESH)
        return carry

    lax.fori_loop(1, n, greet, 0)

    def tables(p, carry):
        for user_of, slot_of, span, block in (
            (user_hold, slot_hold, p, me), (user_own, slot_own, me, p)
        ):
            offset = lax.rem(span - block + n, n)
            count = jnp.int32(0)
            named = [jnp.int32(0)] * SLOTS
            for u in range(users):
                hit = lists[span, u, 0] == offset
                for i in range(1, lists.shape[2]):
                    hit = hit | (lists[span, u, i] == offset)
                hit = hit & (block < lens[u])
                slot_of[p, u] = jnp.where(hit, count, SLOTS)
                for s in range(SLOTS):
                    named[s] = jnp.where(hit & (count == s), u, named[s])
                count = count + jnp.where(hit, 1, 0)
            for s in range(SLOTS):
                user_of[p, s] = named[s]
        return carry

    lax.fori_loop(0, n, tables, 0)

    for recv in recvs:
        for p in range(n):
            recv[p, SLOTS] = jnp.zeros((rows, wide), BF16)

    def copy(ph, f, to, slot):
        return pltpu.make_async_remote_copy(
            src_ref=sends.at[ph, f, to],
            dst_ref=recvs[ph * chunks + f].at[slot, pl.ds(0, SLOTS)],
            send_sem=send_sem.at[ph, f, to], recv_sem=recv_sem.at[ph, f, slot],
            device_id={"seq": to}, device_id_type=pl.DeviceIdType.MESH,
        )

    def exchange(ph, f, read, user_of):
        recv = recvs[ph * chunks + f]
        for s in range(SLOTS):
            recv[me, s] = read(user_of[me, s], me)

        def step(d, carry):
            to = lax.rem(me + d, n)
            for s in range(SLOTS):
                sends[ph, f, to, s] = read(user_of[to, s], to)
            copy(ph, f, to, me).start()
            return carry

        lax.fori_loop(1, n, step, 0)

    def arrive(ph, f):
        def step(d, carry):
            source = lax.rem(me + n - d, n)
            copy(ph, f, source, source).wait_recv()
            return carry

        lax.fori_loop(1, n, step, 0)

    def spread(ph, f, slot_of, dense):
        recv = recvs[ph * chunks + f]

        def step(p, carry):
            for u in range(users):
                dense[u, p, :, f * wide:(f + 1) * wide] = recv[p, slot_of[p, u]]
            return carry

        lax.fori_loop(0, n, step, 0)

    def gathered(ph, f, slot_of):
        recv = recvs[ph * chunks + f]
        out = []
        for u in range(users):
            total = recv[0, slot_of[0, u]].astype(F32)
            for p in range(1, n):
                total = total + recv[p, slot_of[p, u]].astype(F32)
            out.append(total)
        return jnp.concatenate(out, axis=0)

    def cols(f):
        return slice(f * wide, (f + 1) * wide)

    def each_pair(f, body):
        def step(i, carry):
            u = i // pairs
            at = pl.multiple_of(f * wide + lax.rem(i, pairs) * PAIR, PAIR)
            body(u, pl.ds(at, PAIR), f * users * pairs + i)
            return carry

        lax.fori_loop(0, users * pairs, step, 0)

    def forward(f):
        arrive(0, f)
        spread(0, f, slot_hold, q_dense)

        def body(u, at, index):
            query = split_heads(q_dense[u, :, :, at].reshape(latents, PAIR))
            for j in range(0, events, TILE):
                half = dot(k_buf[u, j:j + TILE, at], query, NT).astype(BF16)
                bent = jnp.tanh(half)
                up = 1.0 + bent
                weight = half * up
                w_buf[index, j:j + TILE] = weight
                s_buf[index, j:j + TILE] = up + weight * (1.0 - bent)
            a_dense[u, :, :, at] = join_heads(
                dot(vt_buf[u, at, :], w_buf[index], NN)
            ).astype(BF16).reshape(n, rows, PAIR)

        each_pair(f, body)
        exchange(1, f, lambda u, c: a_dense[u, c, :, cols(f)], user_hold)

    lane_a = lax.broadcasted_iota(jnp.int32, (PAIR, PAIR), 0) // HEAD_DIM
    lane_b = lax.broadcasted_iota(jnp.int32, (PAIR, PAIR), 1) // HEAD_DIM
    averager = jnp.where(lane_a == lane_b, 1.0 / HEAD_DIM, 0.0).astype(F32)

    def head_mean(x):
        return lax.dot_general(x, averager, NN, preferred_element_type=F32,
                               precision=lax.Precision.HIGHEST)

    def middle(f):
        arrive(1, f)
        attended_all = gathered(1, f, slot_own)
        for p in range(pairs):
            at = slice(f * wide + p * PAIR, f * wide + (p + 1) * PAIR)
            attended = attended_all[:, p * PAIR:(p + 1) * PAIR]
            gate = small[1, :, :, at].reshape(users * rows, PAIR).astype(F32)
            grad = small[2, :, :, at].reshape(users * rows, PAIR).astype(F32)
            root = lax.rsqrt(head_mean(attended * attended) + EPS)
            normed = attended * root
            logistic = jax.nn.sigmoid(gate)
            gate_silu = gate * logistic
            slope = logistic * (1.0 + gate * (1.0 - logistic))
            shape = (users, rows, PAIR)
            small_out[0, :, :, at] = (normed * gate_silu).astype(BF16).reshape(shape)
            small_out[2, :, :, at] = (grad * normed * slope).astype(BF16).reshape(shape)
            grad_normed = grad * gate_silu
            back = root * (grad_normed - normed * head_mean(grad_normed * normed))
            d_own[:, :, at] = back.astype(BF16).reshape(shape)
        exchange(2, f, lambda u, c: d_own[u, :, cols(f)], user_own)

    def store_copy(i, f, u):
        src, dst = ((k_buf, dkeys), (v_buf, dvalues))[i]
        return pltpu.make_async_copy(
            src.at[u, :, cols(f)], dst.at[u, :, cols(f)], store_sem.at[i, f, u])

    def backward(f):
        arrive(2, f)
        spread(2, f, slot_hold, d_dense)

        def body(u, at, index):
            query = split_heads(q_dense[u, :, :, at].reshape(latents, PAIR))
            grad = split_heads(d_dense[u, :, :, at].reshape(latents, PAIR))
            for j in range(0, events, TILE):
                tile = slice(j, j + TILE)
                grad_weight = dot(v_buf[u, tile, at], grad, NT).astype(BF16)
                grad_score = grad_weight * s_buf[index, tile]
                s_buf[index, tile] = grad_score
                v_buf[u, tile, at] = dot(w_buf[index, tile], grad, NN).astype(BF16)
                k_buf[u, tile, at] = dot(grad_score, query, NN).astype(BF16)
            g_dense[u, :, :, at] = (
                join_heads(dot(kt_buf[u, at, :], s_buf[index], NN)) * 0.0625
            ).astype(BF16).reshape(n, rows, PAIR)

        each_pair(f, body)
        exchange(3, f, lambda u, c: g_dense[u, c, :, cols(f)], user_hold)
        for u in range(users):
            store_copy(0, f, u).start()
            store_copy(1, f, u).start()

    def finish(f):
        arrive(3, f)
        small_out[1, :, :, cols(f)] = gathered(3, f, slot_own).astype(BF16).reshape(
            users, rows, wide)

    pl.semaphore_wait(barrier, n - 1)
    for f in range(chunks):
        exchange(0, f, lambda u, c: (small[0, u, :, cols(f)] * 0.0625).astype(BF16), user_own)

    for u in range(users):
        load_copy(0, u).wait()
        load_copy(1, u).wait()

    def flip(i, carry):
        u = i // (width // PAIR)
        at = pl.ds(pl.multiple_of(lax.rem(i, width // PAIR) * PAIR, PAIR), PAIR)
        kt_buf[u, at, :] = k_buf[u, :, at].T
        vt_buf[u, at, :] = v_buf[u, :, at].T
        return carry

    lax.fori_loop(0, users * (width // PAIR), flip, 0)

    forward(0)
    for f in range(1, chunks):
        forward(f)
        middle(f - 1)
    for f in range(chunks):
        if f == chunks - 1:
            middle(chunks - 1) if chunks == 1 else None
        backward(f)
        if f == 0 and chunks > 1:
            middle(chunks - 1)
    for f in range(chunks):
        finish(f)

    for ph in range(4):
        for f in range(chunks):
            def drain(d, carry):
                to = lax.rem(me + d, n)
                copy(ph, f, to, me).wait_send()
                return carry

            lax.fori_loop(1, n, drain, 0)
    for f in range(chunks):
        for u in range(users):
            store_copy(0, f, u).wait()
            store_copy(1, f, u).wait()


def body(n, chunks, queries, gate_pre, event_keys, event_values, block_lists, history_len, out_grad):
    rows, users, width = queries.shape
    events = event_keys.shape[0]
    small = jnp.stack([queries, gate_pre, out_grad]).transpose(0, 2, 1, 3)
    keys = event_keys.transpose(1, 0, 2)
    values = event_values.transpose(1, 0, 2)
    wide = width // chunks
    latents = n * rows
    pair_count = users * width // PAIR
    vmem = pl.BlockSpec(memory_space=pltpu.VMEM)
    smem = pl.BlockSpec(memory_space=pltpu.SMEM)
    hbm = pl.BlockSpec(memory_space=pl.ANY)
    table = [pltpu.SMEM((n, SLOTS), jnp.int32), pltpu.SMEM((n, users), jnp.int32)]
    flops = 6 * 2 * users * width * latents * events
    small_out, dkeys, dvalues = pl.pallas_call(
        functools.partial(kernel, n, chunks),
        out_shape=(
            jax.ShapeDtypeStruct((3, users, rows, width), BF16),
            jax.ShapeDtypeStruct((users, events, width), BF16),
            jax.ShapeDtypeStruct((users, events, width), BF16),
        ),
        in_specs=[smem, smem, vmem, hbm, hbm],
        out_specs=(vmem, hbm, hbm),
        scratch_shapes=[
            pltpu.VMEM((users, events, width), BF16),
            pltpu.VMEM((users, events, width), BF16),
            pltpu.VMEM((users, width, events), BF16),
            pltpu.VMEM((users, width, events), BF16),
            pltpu.VMEM((pair_count, events, 2 * latents), BF16),
            pltpu.VMEM((pair_count, events, 2 * latents), BF16),
            pltpu.VMEM((users, n, rows, width), BF16),
            pltpu.VMEM((users, n, rows, width), BF16),
            pltpu.VMEM((users, n, rows, width), BF16),
            pltpu.VMEM((users, n, rows, width), BF16),
            pltpu.VMEM((users, rows, width), BF16),
            pltpu.VMEM((4, chunks, n, SLOTS, rows, wide), BF16),
            (pltpu.VMEM((n, SLOTS + 1, rows, wide), BF16),) * (4 * chunks),
            *table,
            *table,
            pltpu.SemaphoreType.DMA((4, chunks, n)),
            pltpu.SemaphoreType.DMA((4, chunks, n)),
            pltpu.SemaphoreType.DMA((2, users)),
            pltpu.SemaphoreType.DMA((2, chunks, users)),
        ],
        compiler_params=pltpu.CompilerParams(
            collective_id=0, has_side_effects=True, vmem_limit_bytes=62 * 1024 * 1024
        ),
        cost_estimate=pl.CostEstimate(
            flops=flops, bytes_accessed=8 * users * events * width, transcendentals=0),
        name="sparse_attention",
    )(block_lists, history_len, small, keys, values)
    small_out = small_out.transpose(0, 2, 1, 3)
    return (
        small_out[0],
        small_out[1],
        small_out[2],
        dkeys.transpose(1, 0, 2),
        dvalues.transpose(1, 0, 2),
    )


def solution(mesh):
    shard = P("seq", "dp", "head")
    return jax.shard_map(
        functools.partial(body, mesh.shape["seq"], 2),
        mesh=mesh,
        in_specs=(shard, shard, shard, shard, P(None, "dp", None), P("dp"), shard),
        out_specs=(shard,) * 5,
        check_vma=False,
    )
```

profile of v0, /device:TPU:0, one launch (start us, length us, event | category | flops | bytes accessed | tf_op | source)
XLA Modules:
  0.0 82.7 jit_solution(16517974053019400753)
XLA Ops:
  0.6 1.4 %copy.17.lists = s32[8,4,4]{2,1,0:T(4,128)} copy(s32[8,4,4]{0,2,1:T(4,128)} %param.11) | data formatting | bytes 1024 | tf_op args[4]
  2.0 0.9 %copy.28 = bf16[16,4,512]{2,0,1:T(8,128)(2,1)S(1)} copy(bf16[16,4,512]{2,1,0:T(4,128)(2,1)} %param.7) | data formatting | bytes 131072 | tf_op args[0]
  2.9 0.9 %copy_bitcast_fusion.2 = (bf16[1,16,4,512]{3,1,2,0:T(8,128)(2,1)S(1)}, bf16[1,16,4,512]{3,1,2,0:T(8,128)(2,1)S(1)}) fusion(bf16[16,4,512]{2,1,0:T(4,128)(2,1)} %param.13, bf16[16,4,512]{2,1,0:T(4,128)(2,1)} %param.8), kind=kLoop, calls=%fused_computation.6 | loop fusion | bytes 262144 | tf_op jit(solution)/shard_map/stack | solution.py:285
  3.8 0.7 maximum_bitcast_fusion.small
  4.5 7.6 %copy_bitcast_fusion = (bf16[4,1024,512]{2,1,0:T(8,128)(2,1)}, bf16[4,1024,512]{2,1,0:T(8,128)(2,1)}) fusion(bf16[1024,4,512]{2,1,0:T(4,128)(2,1)} %param.10, bf16[1024,4,512]{2,1,0:T(4,128)(2,1)} %param.9), kind=kLoop, calls=%fused_computation | loop fusion | bytes 16777216 | tf_op jit(solution)/shard_map/transpose | solution.py:287
  12.1 55.7 %sparse_attention.1 = (bf16[3,4,16,512]{3,2,1,0:T(8,128)(2,1)}, bf16[4,1024,512]{2,1,0:T(8,128)(2,1)}, bf16[4,1024,512]{2,1,0:T(8,128)(2,1)}) custom-call(s32[8,4,4]{2,1,0:T(4,128)} %copy.17.lists, s32[4]{0:T(128)} %lens.1, bf16[3,4,16,512]{3,2,1,0:T(8,128)(2,1)} %maximum_bitcast_fusion.small, bf16[4,1024,512]{2,1,0:T(8,128)(2,1)} %get-tuple-element.22.keys, ...), custom_call_target="tpu_custom_call" | custom-call | flops 3221225472 | bytes 16777216 | tf_op jit(solution)/shard_map/sparse_attention/pallas_call | solution.py:296
  67.8 0.0 copy-start.1
  67.8 0.0 copy-start
  67.8 7.6 %copy.21 = bf16[1024,4,512]{2,1,0:T(4,128)(2,1)} copy(bf16[1024,4,512]{2,0,1:T(8,128)(2,1)} %bitcast.23) | data formatting | bytes 8388608
  75.4 0.0 copy-done.1
  75.4 0.7 copy.20
  76.1 0.7 copy.19
  76.8 0.7 copy.18
  77.5 0.0 copy-done
  77.5 5.2 %copy.22 = bf16[1024,4,512]{2,1,0:T(4,128)(2,1)} copy(bf16[1024,4,512]{2,0,1:T(8,128)(2,1)S(1)} %bitcast.22) | data formatting | bytes 8388608
  (1 shorter events, 0.0 us)
Async XLA Ops:
  67.8 7.6 %copy-start.1 = (bf16[3,4,16,512]{3,2,1,0:T(8,128)(2,1)S(1)}, bf16[3,4,16,512]{3,2,1,0:T(8,128)(2,1)}, u32[]{:S(2)}) copy-start(bf16[3,4,16,512]{3,2,1,0:T(8,128)(2,1)} %get-tuple-element.8) | copy-start | bytes 589828
  67.8 9.7 %copy-start = (bf16[4,1024,512]{2,1,0:T(8,128)(2,1)S(1)}, bf16[4,1024,512]{2,1,0:T(8,128)(2,1)}, u32[]{:S(2)}) copy-start(bf16[4,1024,512]{2,1,0:T(8,128)(2,1)} %get-tuple-element.10) | copy-start | bytes 12582916
where the time goes:
time: 83 us; the launch traced here: 82.7 us
  Pallas kernels  55.7 us (67%)
  local copies, waits for them, and re-layouts  25.7 us (31%)
    pallas_call x1, Pallas kernels, body(): pl.pallas_call(functools.partial(kernel, n, chunks), out_shape=(jax.Shape...  55.7 us
    unnamed x11, local copies, waits for them, and re-layouts  17.1 us
    transpose x1, local copies, waits for them, and re-layouts, body(): values = event_values.transpose(1, 0, 2)  7.6 us

commit v1 on v0

--- a/solution.py
+++ b/solution.py
@@ -12,6 +12,7 @@
 SLOTS = 2
 PAIR = 2 * HEAD_DIM
 TILE = 256
+GROUP = 64
 F32 = jnp.float32
 BF16 = jnp.bfloat16
 NT = (((1,), (1,)), ((), ()))
@@ -35,25 +36,28 @@
     return jnp.concatenate([flipped[:HEAD_DIM, :half], flipped[HEAD_DIM:, half:]], axis=0).T
 
 
-def kernel(n, chunks, lists, lens, small, keys, values, small_out, dkeys, dvalues,
-           k_buf, v_buf, kt_buf, vt_buf, w_buf, s_buf, q_dense, d_dense, a_dense, g_dense, d_own,
+def kernel(n, chunks, lists, lens, queries, gates, grads, keys, values,
+           out_rows, query_grads, gate_grads, dkeys, dvalues, raw, small, small_out, k_buf, v_buf, kt_buf, vt_buf, w_buf, s_buf, q_dense, d_dense, a_dense, d_own,
            sends, recvs,
            user_hold, slot_hold, user_own, slot_own,
            send_sem, recv_sem, load_sem, store_sem):
     users, events, width = k_buf.shape
-    rows = small.shape[2]
+    rows = queries.shape[0]
     wide = width // chunks
     pairs = wide // PAIR
     latents = n * rows
     me = lax.axis_index("seq")
 
-    def load_copy(i, u):
-        src, dst = ((keys, k_buf), (values, v_buf))[i]
-        return pltpu.make_async_copy(src.at[u], dst.at[u], load_sem.at[i, u])
-
-    for u in range(users):
-        load_copy(0, u).start()
-        load_copy(1, u).start()
+    def cols(f):
+        return slice(f * wide, (f + 1) * wide)
+
+    def load_copy(i, f):
+        return pltpu.make_async_copy(
+            (keys, values)[i].at[:, :, cols(f)], raw.at[i, f % 2], load_sem.at[i, f])
+
+    for f in range(min(2, chunks)):
+        load_copy(0, f).start()
+        load_copy(1, f).start()
 
     barrier = pltpu.get_barrier_semaphore()
 
@@ -64,17 +68,17 @@
 
     lax.fori_loop(1, n, greet, 0)
 
-    def tables(p, carry):
+    def tables(own, p, carry):
         for user_of, slot_of, span, block in (
-            (user_hold, slot_hold, p, me), (user_own, slot_own, me, p)
+            ((user_own, slot_own, me, p),) if own else ((user_hold, slot_hold, p, me),)
         ):
             offset = lax.rem(span - block + n, n)
             count = jnp.int32(0)
             named = [jnp.int32(0)] * SLOTS
             for u in range(users):
-                hit = lists[span, u, 0] == offset
-                for i in range(1, lists.shape[2]):
-                    hit = hit | (lists[span, u, i] == offset)
+                hit = lists[u, 0, span] == offset
+                for i in range(1, lists.shape[1]):
+                    hit = hit | (lists[u, i, span] == offset)
                 hit = hit & (block < lens[u])
                 slot_of[p, u] = jnp.where(hit, count, SLOTS)
                 for s in range(SLOTS):
@@ -84,7 +88,8 @@
                 user_of[p, s] = named[s]
         return carry
 
-    lax.fori_loop(0, n, tables, 0)
+    lax.fori_loop(0, n, functools.partial(tables, True), 0)
+    small[0] = (jnp.swapaxes(queries[...], 0, 1) * 0.0625).astype(BF16)
 
     for recv in recvs:
         for p in range(n):
@@ -139,9 +144,6 @@
                 total = total + recv[p, slot_of[p, u]].astype(F32)
             out.append(total)
         return jnp.concatenate(out, axis=0)
-
-    def cols(f):
-        return slice(f * wide, (f + 1) * wide)
 
     def each_pair(f, body):
         def step(i, carry):
@@ -201,10 +203,28 @@
             d_own[:, :, at] = back.astype(BF16).reshape(shape)
         exchange(2, f, lambda u, c: d_own[u, :, cols(f)], user_own)
 
-    def store_copy(i, f, u):
-        src, dst = ((k_buf, dkeys), (v_buf, dvalues))[i]
+    def store_copy(i, f):
         return pltpu.make_async_copy(
-            src.at[u, :, cols(f)], dst.at[u, :, cols(f)], store_sem.at[i, f, u])
+            raw.at[i, f % 2], (dkeys, dvalues)[i].at[:, :, cols(f)], store_sem.at[i, f])
+
+    def prepare(f):
+        for i, buf in enumerate((k_buf, v_buf)):
+            load_copy(i, f).wait()
+
+            def split(g, carry):
+                at = pl.ds(pl.multiple_of(g * GROUP, GROUP), GROUP)
+                buf[:, at, cols(f)] = jnp.swapaxes(raw[i, f % 2, at], 0, 1)
+                return carry
+
+            lax.fori_loop(0, events // GROUP, split, 0)
+            if f + 2 < chunks:
+                load_copy(i, f + 2).start()
+
+        def flip(u, at, index):
+            kt_buf[u, at, :] = k_buf[u, :, at].T
+            vt_buf[u, at, :] = v_buf[u, :, at].T
+
+        each_pair(f, flip)
 
     def backward(f):
         arrive(2, f)
@@ -220,15 +240,23 @@
                 s_buf[index, tile] = grad_score
                 v_buf[u, tile, at] = dot(w_buf[index, tile], grad, NN).astype(BF16)
                 k_buf[u, tile, at] = dot(grad_score, query, NN).astype(BF16)
-            g_dense[u, :, :, at] = (
+            a_dense[u, :, :, at] = (
                 join_heads(dot(kt_buf[u, at, :], s_buf[index], NN)) * 0.0625
             ).astype(BF16).reshape(n, rows, PAIR)
 
         each_pair(f, body)
-        exchange(3, f, lambda u, c: g_dense[u, c, :, cols(f)], user_hold)
-        for u in range(users):
-            store_copy(0, f, u).start()
-            store_copy(1, f, u).start()
+        exchange(3, f, lambda u, c: a_dense[u, c, :, cols(f)], user_hold)
+        for i, buf in enumerate((k_buf, v_buf)):
+            if f >= 2:
+                store_copy(i, f - 2).wait()
+
+            def merge(g, carry):
+                at = pl.ds(pl.multiple_of(g * GROUP, GROUP), GROUP)
+                raw[i, f % 2, at] = jnp.swapaxes(buf[:, at, cols(f)], 0, 1)
+                return carry
+
+            lax.fori_loop(0, events // GROUP, merge, 0)
+            store_copy(i, f).start()
 
     def finish(f):
         arrive(3, f)
@@ -237,33 +265,29 @@
 
     pl.semaphore_wait(barrier, n - 1)
     for f in range(chunks):
-        exchange(0, f, lambda u, c: (small[0, u, :, cols(f)] * 0.0625).astype(BF16), user_own)
-
-    for u in range(users):
-        load_copy(0, u).wait()
-        load_copy(1, u).wait()
-
-    def flip(i, carry):
-        u = i // (width // PAIR)
-        at = pl.ds(pl.multiple_of(lax.rem(i, width // PAIR) * PAIR, PAIR), PAIR)
-        kt_buf[u, at, :] = k_buf[u, :, at].T
-        vt_buf[u, at, :] = v_buf[u, :, at].T
-        return carry
-
-    lax.fori_loop(0, users * (width // PAIR), flip, 0)
-
+        exchange(0, f, lambda u, c: small[0, u, :, cols(f)], user_own)
+
+    small[1] = jnp.swapaxes(gates[...], 0, 1)
+    small[2] = jnp.swapaxes(grads[...], 0, 1)
+    lax.fori_loop(0, n, functools.partial(tables, False), 0)
+
+    prepare(0)
     forward(0)
     for f in range(1, chunks):
+        prepare(f)
         forward(f)
         middle(f - 1)
+    if chunks == 1:
+        middle(0)
     for f in range(chunks):
-        if f == chunks - 1:
-            middle(chunks - 1) if chunks == 1 else None
         backward(f)
         if f == 0 and chunks > 1:
             middle(chunks - 1)
-    for f in range(chunks):
-        finish(f)
+        if f > 0:
+            finish(f - 1)
+    finish(chunks - 1)
+    for ref, i in ((out_rows, 0), (query_grads, 1), (gate_grads, 2)):
+        ref[...] = jnp.swapaxes(small_out[i], 0, 1)
 
     for ph in range(4):
         for f in range(chunks):
@@ -273,18 +297,14 @@
                 return carry
 
             lax.fori_loop(1, n, drain, 0)
-    for f in range(chunks):
-        for u in range(users):
-            store_copy(0, f, u).wait()
-            store_copy(1, f, u).wait()
+    for f in range(max(0, chunks - 2), chunks):
+        store_copy(0, f).wait()
+        store_copy(1, f).wait()
 
 
 def body(n, chunks, queries, gate_pre, event_keys, event_values, block_lists, history_len, out_grad):
     rows, users, width = queries.shape
     events = event_keys.shape[0]
-    small = jnp.stack([queries, gate_pre, out_grad]).transpose(0, 2, 1, 3)
-    keys = event_keys.transpose(1, 0, 2)
-    values = event_values.transpose(1, 0, 2)
     wide = width // chunks
     latents = n * rows
     pair_count = users * width // PAIR
@@ -293,23 +313,25 @@
     hbm = pl.BlockSpec(memory_space=pl.ANY)
     table = [pltpu.SMEM((n, SLOTS), jnp.int32), pltpu.SMEM((n, users), jnp.int32)]
     flops = 6 * 2 * users * width * latents * events
-    small_out, dkeys, dvalues = pl.pallas_call(
+    return pl.pallas_call(
         functools.partial(kernel, n, chunks),
         out_shape=(
-            jax.ShapeDtypeStruct((3, users, rows, width), BF16),
-            jax.ShapeDtypeStruct((users, events, width), BF16),
-            jax.ShapeDtypeStruct((users, events, width), BF16),
+            *(jax.ShapeDtypeStruct((rows, users, width), BF16),) * 3,
+            jax.ShapeDtypeStruct((events, users, width), BF16),
+            jax.ShapeDtypeStruct((events, users, width), BF16),
         ),
-        in_specs=[smem, smem, vmem, hbm, hbm],
-        out_specs=(vmem, hbm, hbm),
+        in_specs=[smem, smem, vmem, vmem, vmem, hbm, hbm],
+        out_specs=(vmem, vmem, vmem, hbm, hbm),
         scratch_shapes=[
+            pltpu.VMEM((2, 2, events, users, wide), BF16),
+            pltpu.VMEM((3, users, rows, width), BF16),
+            pltpu.VMEM((3, users, rows, width), BF16),
             pltpu.VMEM((users, events, width), BF16),
             pltpu.VMEM((users, events, width), BF16),
             pltpu.VMEM((users, width, events), BF16),
             pltpu.VMEM((users, width, events), BF16),
             pltpu.VMEM((pair_count, events, 2 * latents), BF16),
             pltpu.VMEM((pair_count, events, 2 * latents), BF16),
-            pltpu.VMEM((users, n, rows, width), BF16),
             pltpu.VMEM((users, n, rows, width), BF16),
             pltpu.VMEM((users, n, rows, width), BF16),
             pltpu.VMEM((users, n, rows, width), BF16),
@@ -320,8 +342,8 @@
             *table,
             pltpu.SemaphoreType.DMA((4, chunks, n)),
             pltpu.SemaphoreType.DMA((4, chunks, n)),
-            pltpu.SemaphoreType.DMA((2, users)),
-            pltpu.SemaphoreType.DMA((2, chunks, users)),
+            pltpu.SemaphoreType.DMA((2, chunks)),
+            pltpu.SemaphoreType.DMA((2, chunks)),
         ],
         compiler_params=pltpu.CompilerParams(
             collective_id=0, has_side_effects=True, vmem_limit_bytes=62 * 1024 * 1024
@@ -329,21 +351,14 @@
         cost_estimate=pl.CostEstimate(
             flops=flops, bytes_accessed=8 * users * events * width, transcendentals=0),
         name="sparse_attention",
-    )(block_lists, history_len, small, keys, values)
-    small_out = small_out.transpose(0, 2, 1, 3)
-    return (
-        small_out[0],
-        small_out[1],
-        small_out[2],
-        dkeys.transpose(1, 0, 2),
-        dvalues.transpose(1, 0, 2),
-    )
+    )(block_lists.transpose(1, 2, 0), history_len, queries, gate_pre, out_grad,
+      event_keys, event_values)
 
 
 def solution(mesh):
     shard = P("seq", "dp", "head")
     return jax.shard_map(
-        functools.partial(body, mesh.shape["seq"], 2),
+        functools.partial(body, mesh.shape["seq"], 4),
         mesh=mesh,
         in_specs=(shard, shard, shard, shard, P(None, "dp", None), P("dp"), shard),
         out_specs=(shard,) * 5,

time: 83 us -> 71.4 us (0.86)
  local copies, waits for them, and re-layouts: 25.7 us -> 12.3 us
  Pallas kernels: 55.7 us -> 58.2 us
    transpose x1 -> x0, local copies, waits for them, and re-layouts: 7.6 us -> none  [body(): values = event_values.transpose(1, 0, 2)]
    unnamed x11 -> x7, local copies, waits for them, and re-layouts: 17.1 us -> 12.3 us
    pallas_call x1, Pallas kernels: 55.7 us -> 58.2 us  [body(): pl.pallas_call(functools.partial(kernel, n, chunks), out_shape=(*(jax.Sha...]
    another operation x1 -> x0, local copies, waits for them, and re-layouts: 0.9 us -> none  [body(): small = jnp.stack([queries, gate_pre, out_grad]).transpose(0, 2, 1, 3)]
where the time goes in v1:
time: 71.4 us; the launch traced here: 71.1 us
  Pallas kernels  58.2 us (82%)
  local copies, waits for them, and re-layouts  12.3 us (17%)
    pallas_call x1, Pallas kernels, body(): pl.pallas_call(functools.partial(kernel, n, chunks), out_shape=(*(jax.Sha...  58.2 us
    unnamed x7, local copies, waits for them, and re-layouts  12.3 us

profile of v1, /device:TPU:0, one launch (start us, length us, event | category | flops | bytes accessed | tf_op | source)
XLA Modules:
  0.0 71.1 jit_solution(15577144647867202376)
XLA Ops:
  0.6 58.2 %sparse_attention.1 = (bf16[16,4,512]{2,1,0:T(4,128)(2,1)}, bf16[16,4,512]{2,1,0:T(4,128)(2,1)}, bf16[16,4,512]{2,1,0:T(4,128)(2,1)}, bf16[1024,4,512]{2,1,0:T(4,128)(2,1)}, bf16[1024,4,512]{2,1,0:T(4,128)(2,1)}) custom-call(s32[4,4,8]{2,1,0:T(4,128)} %bitcast.1, s32[4]{0:T(128)} %lens.1, bf16[16,4,512]{2,1,0:T(4,128)(2,1)} %queries.1, ...), custom_call_target="tpu_custom_call" | custom-call | flops 3221225472 | bytes 16777216 | tf_op jit(solution)/shard_map/sparse_attention/pallas_call | solution.py:316
  58.8 1.5 %copy.17 = bf16[16,4,512]{2,1,0:T(4,128)(2,1)} copy(bf16[16,4,512]{2,1,0:T(4,128)(2,1)} %get-tuple-element.10) | data formatting | bytes 131072
  60.3 1.5 %copy.18 = bf16[16,4,512]{2,1,0:T(4,128)(2,1)} copy(bf16[16,4,512]{2,1,0:T(4,128)(2,1)} %get-tuple-element.11) | data formatting | bytes 131072
  61.8 1.5 %copy.19 = bf16[16,4,512]{2,1,0:T(4,128)(2,1)} copy(bf16[16,4,512]{2,1,0:T(4,128)(2,1)} %get-tuple-element.12) | data formatting | bytes 131072
  63.3 0.0 copy-start
  63.3 5.8 %copy.20 = bf16[1024,4,512]{2,1,0:T(4,128)(2,1)} copy(bf16[1024,4,512]{2,1,0:T(4,128)(2,1)} %get-tuple-element.13) | data formatting | bytes 8388608
  69.1 0.0 copy-done
  69.1 2.0 %copy.21 = bf16[1024,4,512]{2,1,0:T(4,128)(2,1)} copy(bf16[1024,4,512]{2,1,0:T(4,128)(2,1)S(1)} %copy-done) | data formatting | bytes 8388608
Async XLA Ops:
  63.3 5.8 %copy-start = (bf16[1024,4,512]{2,1,0:T(4,128)(2,1)S(1)}, bf16[1024,4,512]{2,1,0:T(4,128)(2,1)}, u32[]{:S(2)}) copy-start(bf16[1024,4,512]{2,1,0:T(4,128)(2,1)} %get-tuple-element.14) | copy-start | bytes 12582916

commit v2 on v1

--- a/solution.py
+++ b/solution.py
@@ -37,7 +37,7 @@
 
 
 def kernel(n, chunks, lists, lens, queries, gates, grads, keys, values,
-           out_rows, query_grads, gate_grads, dkeys, dvalues, raw, small, small_out, k_buf, v_buf, kt_buf, vt_buf, w_buf, s_buf, q_dense, d_dense, a_dense, d_own,
+           small_out, dkeys, dvalues, raw, small, k_buf, v_buf, kt_buf, vt_buf, w_buf, s_buf, q_dense, d_dense, a_dense, d_own,
            sends, recvs,
            user_hold, slot_hold, user_own, slot_own,
            send_sem, recv_sem, load_sem, store_sem):
@@ -286,8 +286,6 @@
         if f > 0:
             finish(f - 1)
     finish(chunks - 1)
-    for ref, i in ((out_rows, 0), (query_grads, 1), (gate_grads, 2)):
-        ref[...] = jnp.swapaxes(small_out[i], 0, 1)
 
     for ph in range(4):
         for f in range(chunks):
@@ -313,18 +311,17 @@
     hbm = pl.BlockSpec(memory_space=pl.ANY)
     table = [pltpu.SMEM((n, SLOTS), jnp.int32), pltpu.SMEM((n, users), jnp.int32)]
     flops = 6 * 2 * users * width * latents * events
-    return pl.pallas_call(
+    small_out, dkeys, dvalues = pl.pallas_call(
         functools.partial(kernel, n, chunks),
         out_shape=(
-            *(jax.ShapeDtypeStruct((rows, users, width), BF16),) * 3,
+            jax.ShapeDtypeStruct((3, users, rows, width), BF16),
             jax.ShapeDtypeStruct((events, users, width), BF16),
             jax.ShapeDtypeStruct((events, users, width), BF16),
         ),
         in_specs=[smem, smem, vmem, vmem, vmem, hbm, hbm],
-        out_specs=(vmem, vmem, vmem, hbm, hbm),
+        out_specs=(vmem, hbm, hbm),
         scratch_shapes=[
             pltpu.VMEM((2, 2, events, users, wide), BF16),
-            pltpu.VMEM((3, users, rows, width), BF16),
             pltpu.VMEM((3, users, rows, width), BF16),
             pltpu.VMEM((users, events, width), BF16),
             pltpu.VMEM((users, events, width), BF16),
@@ -353,6 +350,8 @@
         name="sparse_attention",
     )(block_lists.transpose(1, 2, 0), history_len, queries, gate_pre, out_grad,
       event_keys, event_values)
+    small_out = small_out.transpose(0, 2, 1, 3)
+    return small_out[0], small_out[1], small_out[2], dkeys, dvalues
 
 
 def solution(mesh):

time: 71.4 us -> 69.8 us (0.978)
  local copies, waits for them, and re-layouts: 12.3 us -> 10.8 us
    unnamed x7, local copies, waits for them, and re-layouts: 12.3 us -> 9.85 us
    squeeze x0 -> x1, local copies, waits for them, and re-layouts: none -> 0.92 us  [body(): return (small_out[0], small_out[1], small_out[2], dkeys, dvalues)]
where the time goes in v2:
time: 69.8 us; the launch traced here: 69.6 us
  Pallas kernels  58.1 us (83%)
  local copies, waits for them, and re-layouts  10.8 us (15%)
    pallas_call x1, Pallas kernels, body(): pl.pallas_call(functools.partial(kernel, n, chunks), out_shape=(jax.Shape...  58.1 us
    unnamed x7, local copies, waits for them, and re-layouts  9.85 us

profile of v2, /device:TPU:0, one launch (start us, length us, event | category | flops | bytes accessed | tf_op | source)
XLA Modules:
  0.0 69.6 jit_solution(9026023476896135250)
XLA Ops:
  0.6 58.1 %sparse_attention.1 = (bf16[3,4,16,512]{3,2,1,0:T(8,128)(2,1)}, bf16[1024,4,512]{2,1,0:T(4,128)(2,1)}, bf16[1024,4,512]{2,1,0:T(4,128)(2,1)}) custom-call(s32[4,4,8]{2,1,0:T(4,128)} %bitcast.9, s32[4]{0:T(128)} %lens.1, bf16[16,4,512]{2,1,0:T(4,128)(2,1)} %queries.1, bf16[16,4,512]{2,1,0:T(4,128)(2,1)} %gates.1, bf16[16,4,512]{2,1,0:T(4,128)(2,1)} %grads.1, ...), custom_call_target="tpu_custom_call" | custom-call | flops 3221225472 | bytes 16777216 | tf_op jit(solution)/shard_map/sparse_attention/pallas_call | solution.py:314
  58.8 0.9 %slice_bitcast_fusion = (bf16[16,4,512]{2,0,1:T(8,128)(2,1)S(1)}, bf16[16,4,512]{2,0,1:T(8,128)(2,1)S(1)}, bf16[16,4,512]{2,0,1:T(8,128)(2,1)S(1)}) fusion(bf16[3,16,4,512]{3,1,2,0:T(8,128)(2,1)} %bitcast.8), kind=kLoop, calls=%fused_computation | loop fusion | bytes 393216 | tf_op jit(solution)/shard_map/squeeze | solution.py:354
  59.7 0.7 copy.14
  60.4 0.7 copy.13
  61.1 0.7 copy.12
  61.8 0.0 copy-start
  61.8 5.8 %copy.17 = bf16[1024,4,512]{2,1,0:T(4,128)(2,1)} copy(bf16[1024,4,512]{2,1,0:T(4,128)(2,1)} %get-tuple-element.27) | data formatting | bytes 8388608
  67.5 0.0 copy-done
  67.5 2.0 %copy.18 = bf16[1024,4,512]{2,1,0:T(4,128)(2,1)} copy(bf16[1024,4,512]{2,1,0:T(4,128)(2,1)S(1)} %copy-done) | data formatting | bytes 8388608
Async XLA Ops:
  61.8 5.8 %copy-start = (bf16[1024,4,512]{2,1,0:T(4,128)(2,1)S(1)}, bf16[1024,4,512]{2,1,0:T(4,128)(2,1)}, u32[]{:S(2)}) copy-start(bf16[1024,4,512]{2,1,0:T(4,128)(2,1)} %get-tuple-element.28) | copy-start | bytes 12582916
